TPU v7x, 32 devices: a whole 2x2x4 slice. The times are simulated.
32 devices in a mesh: shard: 8 (over z, x), ctx: 2 (over core), tp: 2 (over y).
Axes of the slice: x: 2, y: 2, z: 4, core: 2. Of those that a mesh axis runs over, the one named last changes fastest.
Arguments:
- tokens: bfloat16 [2, 8, 1024, 1280], P(None, 'shard', 'ctx'), may hold values from -6 to 6
- patch_meta: int32 [3, 2, 8, 1024], P(None, None, 'shard'), may hold values from -1 to 31, as said below
- attn_norm_gain: float32 [1280], replicated, may hold values from 0.5 to 1.5
- attn_norm_bias: float32 [1280], replicated, may hold values from -3 to 3
- qkv_weight: bfloat16 [3, 1280, 1280], P(None, 'shard', 'tp'), may hold values from -0.15625 to 0.15625
- qkv_bias: float32 [3, 1280], P(None, 'tp'), may hold values from -3 to 3
- proj_weight: bfloat16 [1280, 1280], P('tp', 'shard'), may hold values from -0.625 to 0.625
- proj_bias: float32 [1280], replicated, may hold values from -3 to 3
- mlp_norm_gain: float32 [1280], replicated, may hold values from 0.5 to 1.5
- mlp_norm_bias: float32 [1280], replicated, may hold values from -3 to 3
- fc1_weight: bfloat16 [1280, 5120], P('shard', 'tp'), may hold values from -0.15625 to 0.15625
- fc1_bias: float32 [5120], P('tp'), may hold values from -3 to 3
- fc2_weight: bfloat16 [5120, 1280], P('tp', 'shard'), may hold values from -0.078125 to 0.078125
- fc2_bias: float32 [1280], replicated, may hold values from -3 to 3
- cotangent: bfloat16 [2, 8, 1024, 1280], P(None, 'shard', 'ctx'), may hold values from -6 to 6
Outputs:
- block_output: bfloat16 [2, 8, 1024, 1280], P(None, 'shard', 'ctx')
- input_grad: float32 [2, 8, 1024, 1280], P(None, 'shard', 'ctx')
- grad_attn_norm_gain: float32 [1280], replicated
- grad_attn_norm_bias: float32 [1280], replicated
- grad_qkv_weight: float32 [3, 1280, 1280], P(None, 'shard', 'tp')
- grad_qkv_bias: float32 [3, 1280], P(None, 'tp')
- grad_proj_weight: float32 [1280, 1280], P('tp', 'shard')
- grad_proj_bias: float32 [1280], replicated
- grad_mlp_norm_gain: float32 [1280], replicated
- grad_mlp_norm_bias: float32 [1280], replicated
- grad_fc1_weight: float32 [1280, 5120], P('shard', 'tp')
- grad_fc1_bias: float32 [5120], P('tp')
- grad_fc2_weight: float32 [5120, 1280], P('tp', 'shard')
- grad_fc2_bias: float32 [1280], replicated
Inputs may be any that keep to these rules, and one draw needn't show every extreme that they name: patch_meta[0] holds each slot's picture id, counting up from 0 along a packed row, and -1 on padding slots, which lie only at a row's end; patch_meta[1] and patch_meta[2] hold the patch's row and column inside its picture (0 on padding). Pictures are rectangles of 10 to 32 patches a side filled row by row; only a row's last picture may have fewer picture rows. Fewer than 32 slots of a row are padding.
All inputs are finite; a program needn't handle non-finite values.
Results may differ from a plain program's by a relative error of at most 0.012.
Values may be sent and summed in bfloat16 or wider, within the bound.
A program may use at most 256 MiB of HBM per device.

v0:
```python
import math
import jax
import jax.numpy as jnp
from jax import lax
from jax.sharding import PartitionSpec as P

HDIM = 80
norm_epsilon = 1e-06
gelu_factor = 1.702
rope_base = 10000.0


def norm_stats(values):
    center = values - jnp.mean(values, -1, keepdims=True)
    spread = jnp.mean(center * center, -1, keepdims=True)
    inverse = lax.rsqrt(spread + norm_epsilon)
    return (center * inverse, inverse)


def norm_back(grad_out, normal, inverse, gain):
    scaled = grad_out * gain
    return inverse * (
        scaled
        - jnp.mean(scaled, -1, keepdims=True)
        - normal * jnp.mean(scaled * normal, -1, keepdims=True)
    )


def rope_tables(patch_row, patch_col, head_size):
    quarter = head_size // 4
    frequency = rope_base ** (-2.0 * jnp.arange(quarter, dtype=jnp.float32) / (head_size // 2))
    angles = jnp.concatenate(
        [
            patch_row.astype(jnp.float32)[:, None] * frequency[None, :],
            patch_col.astype(jnp.float32)[:, None] * frequency[None, :],
        ],
        axis=1,
    )
    angles = jnp.concatenate([angles, angles], axis=1)
    return (jnp.cos(angles)[:, None, :], jnp.sin(angles)[:, None, :])


def rotate_half(tensor):
    half_size = tensor.shape[-1] // 2
    return jnp.concatenate([-tensor[..., half_size:], tensor[..., :half_size]], axis=-1)


def apply_rope(tensor, cosine, sine_table):
    return tensor * cosine + rotate_half(tensor) * sine_table


def undo_rope(gradient, cosine, sine_table):
    return gradient * cosine - rotate_half(gradient * sine_table)


def split_heads(flat, batch, length, head_count):
    return (
        flat.reshape(batch, length, head_count, HDIM)
        .transpose(0, 2, 1, 3)
        .reshape(batch * head_count, length, HDIM)
    )


def join_heads(items, batch, length, head_count):
    return (
        items.reshape(batch, head_count, length, HDIM)
        .transpose(0, 2, 1, 3)
        .reshape(batch, length, head_count * HDIM)
    )


def masked_logits(query_head, key_head, query_ids, key_ids):
    logits = jnp.einsum("qd,kd->qk", query_head, key_head, preferred_element_type=jnp.float32) * (
        1.0 / math.sqrt(HDIM)
    )
    return jnp.where(query_ids[:, None] == key_ids[None, :], logits, -1e30)


def attend(packed):
    query_head, key_head, value_head, query_ids, key_ids = packed
    logits = masked_logits(query_head, key_head, query_ids, key_ids)
    peak = jnp.max(logits, -1, keepdims=True)
    exponent = jnp.exp(logits - peak)
    normalizer = jnp.sum(exponent, -1, keepdims=True)
    probs_low = (exponent / normalizer).astype(jnp.bfloat16)
    mixed_head = jnp.einsum("qk,kd->qd", probs_low, value_head, preferred_element_type=jnp.float32)
    return (mixed_head.astype(jnp.bfloat16), peak[:, 0] + jnp.log(normalizer[:, 0]))


def attend_back(packed):
    query_head, key_head, value_head, query_ids, key_ids, grad_head, log_total = packed
    score_scale = 1.0 / math.sqrt(HDIM)
    logits = masked_logits(query_head, key_head, query_ids, key_ids)
    probs = jnp.exp(logits - log_total[:, None])
    d_probs = jnp.einsum("qd,kd->qk", grad_head, value_head, preferred_element_type=jnp.float32)
    inner_sum = jnp.sum(probs * d_probs, -1, keepdims=True)
    d_logits = (probs * (d_probs - inner_sum)).astype(jnp.bfloat16)
    d_query = (
        jnp.einsum("qk,kd->qd", d_logits, key_head, preferred_element_type=jnp.float32)
        * score_scale
    )
    d_key = (
        jnp.einsum("qk,qd->kd", d_logits, query_head, preferred_element_type=jnp.float32)
        * score_scale
    )
    d_value = jnp.einsum(
        "qk,qd->kd", probs.astype(jnp.bfloat16), grad_head, preferred_element_type=jnp.float32
    )
    return (d_query, d_key, d_value)


def per_device(
    tokens,
    patch_meta,
    attn_norm_gain,
    attn_norm_bias,
    qkv_weight,
    qkv_bias,
    proj_weight,
    proj_bias,
    mlp_norm_gain,
    mlp_norm_bias,
    fc1_weight,
    fc1_bias,
    fc2_weight,
    fc2_bias,
    cotangent,
):
    local_len = tokens.shape[2]
    model_width = tokens.shape[3]
    full_len = patch_meta.shape[3]
    inner_width = qkv_weight.shape[2]
    ff_local = fc1_weight.shape[1]
    head_count = inner_width // HDIM
    offset = lax.axis_index("ctx") * local_len
    full_qkv, full_proj, full_first, full_second = (
        lax.all_gather(qkv_weight, "shard", axis=1, tiled=True),
        lax.all_gather(proj_weight, "shard", axis=1, tiled=True),
        lax.all_gather(fc1_weight, "shard", axis=0, tiled=True),
        lax.all_gather(fc2_weight, "shard", axis=1, tiled=True),
    )

    def one_micro(running, sample):
        tok_one, cot_one, meta_one = sample
        ids_all = meta_one[0]
        ids_own = lax.dynamic_slice_in_dim(ids_all, offset, local_len, 1)
        own_row = lax.dynamic_slice_in_dim(meta_one[1], offset, local_len, 1).reshape(local_len)
        own_col = lax.dynamic_slice_in_dim(meta_one[2], offset, local_len, 1).reshape(local_len)
        cosine, sine_table = rope_tables(own_row, own_col, HDIM)
        inputs = tok_one.reshape(local_len, model_width).astype(jnp.float32)
        normal_one, inverse_one = norm_stats(inputs)
        normed = (normal_one * attn_norm_gain + attn_norm_bias).astype(jnp.bfloat16)
        projected = (
            jnp.einsum("rd,cde->cre", normed, full_qkv, preferred_element_type=jnp.float32)
            + qkv_bias[:, None, :]
        )
        query = apply_rope(
            projected[0].reshape(local_len, head_count, HDIM), cosine, sine_table
        ).astype(jnp.bfloat16)
        key_part = apply_rope(
            projected[1].reshape(local_len, head_count, HDIM), cosine, sine_table
        ).astype(jnp.bfloat16)
        value_part = projected[2].astype(jnp.bfloat16)
        key_all, value_all = (
            lax.all_gather(key_part.reshape(1, local_len, inner_width), "ctx", axis=1, tiled=True),
            lax.all_gather(
                value_part.reshape(1, local_len, inner_width), "ctx", axis=1, tiled=True
            ),
        )
        query_items = split_heads(query, 1, local_len, head_count)
        key_items = split_heads(key_all, 1, full_len, head_count)
        value_items = split_heads(value_all, 1, full_len, head_count)
        query_ids = jnp.repeat(ids_own, head_count, axis=0)
        key_ids = jnp.repeat(ids_all, head_count, axis=0)
        mixed_items, log_totals = lax.map(
            attend, (query_items, key_items, value_items, query_ids, key_ids)
        )
        mixed = join_heads(mixed_items, 1, local_len, head_count).reshape(local_len, inner_width)
        attn_out = (
            lax.psum(jnp.dot(mixed, full_proj, preferred_element_type=jnp.float32), "tp")
            + proj_bias
        )
        hidden = inputs + attn_out
        normal_two, inverse_two = norm_stats(hidden)
        normed_two = (normal_two * mlp_norm_gain + mlp_norm_bias).astype(jnp.bfloat16)
        pre_act = jnp.dot(normed_two, full_first, preferred_element_type=jnp.float32) + fc1_bias
        sigmoid_part = jax.nn.sigmoid(gelu_factor * pre_act)
        activated = (pre_act * sigmoid_part).astype(jnp.bfloat16)
        mlp_out = (
            lax.psum(
                jnp.dot(activated, full_second, preferred_element_type=jnp.float32).astype(
                    jnp.bfloat16
                ),
                "tp",
            ).astype(jnp.float32)
            + fc2_bias
        )
        output_one = (hidden + mlp_out).astype(jnp.bfloat16).reshape(tok_one.shape)
        back_qkv, back_proj, back_first, back_second = (
            lax.all_gather(qkv_weight, "shard", axis=1, tiled=True),
            lax.all_gather(proj_weight, "shard", axis=1, tiled=True),
            lax.all_gather(fc1_weight, "shard", axis=0, tiled=True),
            lax.all_gather(fc2_weight, "shard", axis=1, tiled=True),
        )
        grad_low = cot_one.reshape(local_len, model_width)
        grad_out = grad_low.astype(jnp.float32)
        grad_second = jnp.einsum(
            "rf,rd->fd", activated, grad_low, preferred_element_type=jnp.float32
        )
        grad_second_bias = jnp.sum(grad_out, 0)
        d_act = jnp.einsum("rd,fd->rf", grad_low, back_second, preferred_element_type=jnp.float32)
        d_pre = (
            d_act * (sigmoid_part + gelu_factor * pre_act * sigmoid_part * (1.0 - sigmoid_part))
        ).astype(jnp.bfloat16)
        grad_first = jnp.einsum("rd,rf->df", normed_two, d_pre, preferred_element_type=jnp.float32)
        grad_first_bias = jnp.sum(d_pre.astype(jnp.float32), 0)
        d_norm_two = lax.psum(
            jnp.einsum("rf,df->rd", d_pre, back_first, preferred_element_type=jnp.float32), "tp"
        )
        grad_mlp_gain = jnp.sum(d_norm_two * normal_two, 0)
        grad_mlp_shift = jnp.sum(d_norm_two, 0)
        d_hidden = grad_out + norm_back(d_norm_two, normal_two, inverse_two, mlp_norm_gain)
        d_attn = d_hidden.astype(jnp.bfloat16)
        grad_proj_bias = jnp.sum(d_attn.astype(jnp.float32), 0)
        grad_proj = jnp.einsum("re,rd->ed", mixed, d_attn, preferred_element_type=jnp.float32)
        d_mixed = jnp.einsum(
            "rd,ed->re", d_attn, back_proj, preferred_element_type=jnp.float32
        ).astype(jnp.bfloat16)
        grad_items = split_heads(d_mixed, 1, local_len, head_count)
        d_query_items, d_key_items, d_value_items = lax.map(
            attend_back,
            (query_items, key_items, value_items, query_ids, key_ids, grad_items, log_totals),
        )
        d_key_all = join_heads(d_key_items, 1, full_len, head_count)
        d_value_all = join_heads(d_value_items, 1, full_len, head_count)
        d_key_own, d_value_own = (
            lax.psum_scatter(d_key_all, "ctx", scatter_dimension=1, tiled=True),
            lax.psum_scatter(d_value_all, "ctx", scatter_dimension=1, tiled=True),
        )
        d_query = join_heads(d_query_items, 1, local_len, head_count).reshape(
            local_len, head_count, HDIM
        )
        d_query_raw = undo_rope(d_query, cosine, sine_table).reshape(local_len, inner_width)
        d_key_raw = undo_rope(
            d_key_own.reshape(local_len, head_count, HDIM), cosine, sine_table
        ).reshape(local_len, inner_width)
        d_projected = jnp.stack(
            [d_query_raw, d_key_raw, d_value_own.reshape(local_len, inner_width)]
        ).astype(jnp.bfloat16)
        grad_qkv = jnp.einsum(
            "rd,cre->cde", normed, d_projected, preferred_element_type=jnp.float32
        )
        grad_qkv_shift = jnp.sum(d_projected.astype(jnp.float32), 1)
        d_normed = lax.psum(
            jnp.einsum("cre,cde->rd", d_projected, back_qkv, preferred_element_type=jnp.float32),
            "tp",
        )
        grad_attn_gain = jnp.sum(d_normed * normal_one, 0)
        grad_attn_shift = jnp.sum(d_normed, 0)
        input_one = (
            d_hidden + norm_back(d_normed, normal_one, inverse_one, attn_norm_gain)
        ).reshape(tok_one.shape)
        fresh = (
            grad_qkv,
            grad_proj,
            grad_first,
            grad_second,
            grad_attn_gain,
            grad_attn_shift,
            grad_qkv_shift,
            grad_proj_bias,
            grad_mlp_gain,
            grad_mlp_shift,
            grad_first_bias,
            grad_second_bias,
        )
        running = jax.tree.map(lambda earlier, latest: earlier + latest, running, fresh)
        return (running, (output_one, input_one))

    start_sums = (
        jnp.zeros((3, model_width, inner_width), jnp.float32),
        jnp.zeros((inner_width, model_width), jnp.float32),
        jnp.zeros((model_width, ff_local), jnp.float32),
        jnp.zeros((ff_local, model_width), jnp.float32),
        jnp.zeros((model_width,), jnp.float32),
        jnp.zeros((model_width,), jnp.float32),
        jnp.zeros((3, inner_width), jnp.float32),
        jnp.zeros((model_width,), jnp.float32),
        jnp.zeros((model_width,), jnp.float32),
        jnp.zeros((model_width,), jnp.float32),
        jnp.zeros((ff_local,), jnp.float32),
        jnp.zeros((model_width,), jnp.float32),
    )
    totals, (block_output, input_grad) = lax.scan(
        one_micro, start_sums, (tokens, cotangent, jnp.moveaxis(patch_meta, 1, 0))
    )
    small_sums = lax.psum(
        (totals[4], totals[5], totals[6], totals[7], totals[8], totals[9], totals[10], totals[11]),
        ("shard", "ctx"),
    )
    weight_grads = (totals[0], totals[1], totals[2], totals[3])
    weight_grads = (
        lax.psum_scatter(weight_grads[0], "shard", scatter_dimension=1, tiled=True),
        lax.psum_scatter(weight_grads[1], "shard", scatter_dimension=1, tiled=True),
        lax.psum_scatter(weight_grads[2], "shard", scatter_dimension=0, tiled=True),
        lax.psum_scatter(weight_grads[3], "shard", scatter_dimension=1, tiled=True),
    )
    weight_grads = lax.psum(
        (weight_grads[0], weight_grads[1], weight_grads[2], weight_grads[3]), "ctx"
    )
    return (
        block_output,
        input_grad,
        small_sums[0],
        small_sums[1],
        weight_grads[0],
        small_sums[2],
        weight_grads[1],
        small_sums[3],
        small_sums[4],
        small_sums[5],
        weight_grads[2],
        small_sums[6],
        weight_grads[3],
        small_sums[7],
    )


def solution(mesh):
    placed = (
        P(None, "shard", "ctx", None),
        P(None, None, "shard", None),
        P(),
        P(),
        P(None, "shard", "tp"),
        P(None, "tp"),
        P("tp", "shard"),
        P(),
        P(),
        P(),
        P("shard", "tp"),
        P("tp"),
        P("tp", "shard"),
        P(),
        P(None, "shard", "ctx", None),
    )
    return jax.shard_map(
        per_device,
        mesh=mesh,
        in_specs=placed,
        out_specs=(
            P(None, "shard", "ctx", None),
            P(None, "shard", "ctx", None),
            P(),
            P(),
            P(None, "shard", "tp"),
            P(None, "tp"),
            P("tp", "shard"),
            P(),
            P(),
            P(),
            P("shard", "tp"),
            P("tp"),
            P("tp", "shard"),
            P(),
        ),
        check_vma=False,
    )
```

profile of v0, /device:TPU:0, one launch (start us, length us, event | category | flops | bytes accessed | tf_op | source)
XLA Modules:
  0.0 2368.6 jit_solution(1720924637512056237)
XLA Ops:
  11.7 46.6 %all-gather.13.cloned.1.call-done = bf16[640,1280]{0,1:T(8,128)(2,1)} async-done(((bf16[640,160]{0,1:T(8,128)(2,1)}), bf16[640,1280]{0,1:T(8,128)(2,1)}) %all-gather.13.cloned.1.call-update) | async-done | bytes 1638416 | tf_op jit(solution)/shard_map/all_gather | solution.py:138
  61.9 99.7 %all-gather.17.cloned.1.call-done = bf16[2560,1280]{0,1:T(8,128)(2,1)} async-done(((bf16[2560,160]{0,1:T(8,128)(2,1)}), bf16[2560,1280]{0,1:T(8,128)(2,1)}) %all-gather.17.cloned.1.call-update) | async-done | bytes 6553616 | tf_op jit(solution)/shard_map/all_gather | solution.py:140
  161.6 9.5 copy.94
  171.2 73.1 %all-gather.11.cloned.1.call-done = bf16[3,1280,640]{2,1,0:T(8,128)(2,1)} async-done(((bf16[3,160,640]{2,1,0:T(8,128)(2,1)}), bf16[3,1280,640]{2,1,0:T(8,128)(2,1)}) %all-gather.11.cloned.1.call-update) | async-done | bytes 4915216 | tf_op jit(solution)/shard_map/all_gather | solution.py:137
  244.3 102.5 %all-gather.15.cloned.1.call-done = bf16[1280,2560]{1,0:T(8,128)(2,1)} async-done(((bf16[160,2560]{1,0:T(8,128)(2,1)}), bf16[1280,2560]{1,0:T(8,128)(2,1)}) %all-gather.15.cloned.1.call-update) | async-done | bytes 6553616 | tf_op jit(solution)/shard_map/all_gather | solution.py:139
  346.9 1259.4 %while.96 = (s32[]{:T(128)}, f32[3,1280,640]{1,2,0:T(8,128)}, f32[640,1280]{1,0:T(8,128)}, f32[1280,2560]{1,0:T(8,128)}, f32[2560,1280]{1,0:T(8,128)}, /*index=5...) while((s32[]{:T(128)}, f32[3,1280,640]{1,2,0:T(8,128)}, ...), condition=%wide.region_30.31_spmd.clone, body=%wide.region_0.30_spmd.clone.sunk | while | flops 30925250560 | bytes 610404544 | solution.py:294
  380.2 40.1 %while.97 = (s32[]{:T(128)}, bf16[8,512,80]{1,2,0:T(8,128)(2,1)S(1)}, f32[8,512]{1,0:T(8,128)}, s32[8,512]{1,0:T(8,128)S(1)}, s32[8,1024]{1,0:T(8,128)S(1)}, /*i...) while((s32[]{:T(128)}, ...), condition=%wide.region_6.6_spmd, body=%wide.region_3.5_spmd.sunk | while | flops 172531200 | bytes 7069817 | solution.py:175
  426.4 74.0 %all-reduce.10.cloned.1.call-done = f32[512,1280]{1,0:T(8,128)} async-done(((f32[512,1280]{1,0:T(8,128)}), f32[512,1280]{1,0:T(8,128)}) %all-reduce.10.cloned.1.call-update) | async-done | bytes 2621456 | tf_op jit(solution)/shard_map/while/body/eval_jaxpr/psum | solution.py:180
  503.4 8.4 fusion.165
  511.8 18.7 all-gather.25.cloned.1.call-done
  530.5 11.5 convert_reduce_fusion.10
  542.1 90.7 %all-gather.27.cloned.1.call-done = bf16[1280,2560]{1,0:T(8,128)(2,1)} async-done(((bf16[160,2560]{1,0:T(8,128)(2,1)}), bf16[1280,2560]{1,0:T(8,128)(2,1)}) %all-gather.27.cloned.1.call-update) | async-done | bytes 6553616 | tf_op jit(solution)/shard_map/while/body/eval_jaxpr/all_gather | solution.py:202
  632.7 8.8 fusion.166
  642.1 10.6 convolution_convert_fusion.6
  652.8 10.3 reduce-scatter.15.cloned.1.call-start
  663.1 51.0 %all-reduce.12.cloned.1.call-done = f32[512,1280]{1,0:T(8,128)} async-done(((f32[512,1280]{1,0:T(8,128)}), f32[512,1280]{1,0:T(8,128)}) %all-reduce.12.cloned.1.call-update) | async-done | bytes 2621456 | tf_op jit(solution)/shard_map/while/body/eval_jaxpr/psum | solution.py:217
  725.7 75.7 %while.98 = (s32[]{:T(128)}, f32[8,512,80]{1,2,0:T(8,128)}, f32[8,1024,80]{1,2,0:T(8,128)}, f32[8,1024,80]{1,2,0:T(8,128)}, s32[8,512]{1,0:T(8,128)S(1)}, /*inde...) while((s32[]{:T(128)}, f32[8,512,80]{1,2,0:T(8,128)}, ...), condition=%wide.region_15.15_spmd, body=%wide.region_13.14_spmd.sunk | while | flops 424795648 | bytes 17794184 | solution.py:230
  803.0 12.0 convolution_add_fusion.8
  820.0 5.5 reduce-scatter.17.cloned.1.call-done
  831.1 55.9 %all-gather.29.cloned.1.call-done = bf16[3,1280,640]{2,1,0:T(8,128)(2,1)} async-done(((bf16[3,160,640]{2,1,0:T(8,128)(2,1)}), bf16[3,1280,640]{2,1,0:T(8,128)(2,1)}) %all-gather.29.cloned.1.call-update) | async-done | bytes 4915216 | tf_op jit(solution)/shard_map/while/body/eval_jaxpr/all_gather | solution.py:200
  887.0 7.2 convolution_bitcast_fusion.3
  894.4 9.1 convolution_add_fusion.7
  907.4 6.4 bitcast_add_fusion.2
  913.9 53.1 %all-reduce.14.cloned.1.call-done = f32[512,1280]{1,0:T(8,128)} async-done(((f32[512,1280]{1,0:T(8,128)}), f32[512,1280]{1,0:T(8,128)}) %all-reduce.14.cloned.1.call-update) | async-done | bytes 2621456 | tf_op jit(solution)/shard_map/while/body/eval_jaxpr/psum | solution.py:254
  999.0 6.5 all-gather.19.cloned.1.call-done
  1009.6 40.1 %while.97 = (s32[]{:T(128)}, bf16[8,512,80]{1,2,0:T(8,128)(2,1)S(1)}, f32[8,512]{1,0:T(8,128)}, s32[8,512]{1,0:T(8,128)S(1)}, s32[8,1024]{1,0:T(8,128)S(1)}, /*i...) while((s32[]{:T(128)}, ...), condition=%wide.region_6.6_spmd, body=%wide.region_3.5_spmd.sunk | while | flops 172531200 | bytes 7069817 | solution.py:175
  1055.8 74.0 %all-reduce.10.cloned.1.call-done = f32[512,1280]{1,0:T(8,128)} async-done(((f32[512,1280]{1,0:T(8,128)}), f32[512,1280]{1,0:T(8,128)}) %all-reduce.10.cloned.1.call-update) | async-done | bytes 2621456 | tf_op jit(solution)/shard_map/while/body/eval_jaxpr/psum | solution.py:180
  1132.8 8.4 fusion.165
  1141.2 19.1 all-gather.25.cloned.1.call-done
  1160.2 11.5 convert_reduce_fusion.10
  1171.8 90.8 %all-gather.27.cloned.1.call-done = bf16[1280,2560]{1,0:T(8,128)(2,1)} async-done(((bf16[160,2560]{1,0:T(8,128)(2,1)}), bf16[1280,2560]{1,0:T(8,128)(2,1)}) %all-gather.27.cloned.1.call-update) | async-done | bytes 6553616 | tf_op jit(solution)/shard_map/while/body/eval_jaxpr/all_gather | solution.py:202
  1262.6 8.8 fusion.166
  1272.0 10.6 convolution_convert_fusion.6
  1282.9 61.1 %all-reduce.12.cloned.1.call-done = f32[512,1280]{1,0:T(8,128)} async-done(((f32[512,1280]{1,0:T(8,128)}), f32[512,1280]{1,0:T(8,128)}) %all-reduce.12.cloned.1.call-update) | async-done | bytes 2621456 | tf_op jit(solution)/shard_map/while/body/eval_jaxpr/psum | solution.py:217
  1355.7 75.8 %while.98 = (s32[]{:T(128)}, f32[8,512,80]{1,2,0:T(8,128)}, f32[8,1024,80]{1,2,0:T(8,128)}, f32[8,1024,80]{1,2,0:T(8,128)}, s32[8,512]{1,0:T(8,128)S(1)}, /*inde...) while((s32[]{:T(128)}, f32[8,512,80]{1,2,0:T(8,128)}, ...), condition=%wide.region_15.15_spmd, body=%wide.region_13.14_spmd.sunk | while | flops 424795648 | bytes 17794184 | solution.py:230
  1432.9 16.3 convolution_add_fusion.8
  1461.0 55.6 %all-gather.29.cloned.1.call-done = bf16[3,1280,640]{2,1,0:T(8,128)(2,1)} async-done(((bf16[3,160,640]{2,1,0:T(8,128)(2,1)}), bf16[3,1280,640]{2,1,0:T(8,128)(2,1)}) %all-gather.29.cloned.1.call-update) | async-done | bytes 4915216 | tf_op jit(solution)/shard_map/while/body/eval_jaxpr/all_gather | solution.py:200
  1516.6 7.2 convolution_bitcast_fusion.3
  1524.0 11.9 convolution_add_fusion.7
  1539.9 8.1 bitcast_add_fusion.2
  1548.0 48.6 %all-reduce.14.cloned.1.call-done = f32[512,1280]{1,0:T(8,128)} async-done(((f32[512,1280]{1,0:T(8,128)}), f32[512,1280]{1,0:T(8,128)}) %all-reduce.14.cloned.1.call-update) | async-done | bytes 2621456 | tf_op jit(solution)/shard_map/while/body/eval_jaxpr/psum | solution.py:254
  1611.0 11.3 copy.95
  1623.1 14.0 copy.97
  1637.2 50.0 %reduce-scatter.9.cloned.1.call-done = f32[640,160]{0,1:T(8,128)} async-done(((f32[640,1280]{0,1:T(8,128)}), f32[640,160]{0,1:T(8,128)}) %reduce-scatter.9.cloned.1.call-update) | async-done | bytes 409616 | tf_op jit(solution)/shard_map/reduce_scatter | solution.py:304
  1687.2 171.9 %reduce-scatter.7.cloned.1.call-done = f32[3,160,640]{2,1,0:T(8,128)} async-done(((f32[3,1280,640]{2,1,0:T(8,128)}), f32[3,160,640]{2,1,0:T(8,128)}) %reduce-scatter.7.cloned.1.call-update) | async-done | bytes 1228816 | tf_op jit(solution)/shard_map/reduce_scatter | solution.py:303
  1859.1 217.8 %reduce-scatter.11.cloned.1.call-done = f32[160,2560]{1,0:T(8,128)} async-done(((f32[1280,2560]{1,0:T(8,128)}), f32[160,2560]{1,0:T(8,128)}) %reduce-scatter.11.cloned.1.call-update) | async-done | bytes 1638416 | tf_op jit(solution)/shard_map/reduce_scatter | solution.py:305
  2076.9 217.6 %reduce-scatter.13.cloned.1.call-done = f32[2560,160]{0,1:T(8,128)} async-done(((f32[2560,1280]{0,1:T(8,128)}), f32[2560,160]{0,1:T(8,128)}) %reduce-scatter.13.cloned.1.call-update) | async-done | bytes 1638416 | tf_op jit(solution)/shard_map/reduce_scatter | solution.py:306
  2294.7 61.0 %all-reduce = (f32[1280]{0:T(1024)}, f32[1280]{0:T(1024)}, f32[3,640]{1,0:T(4,128)}, f32[1280]{0:T(1024)}, f32[1280]{0:T(1024)}, /*index=5*/f32[1280]{0:T(1024)}, f32[2560]{0:T(1024)}, f32[1280]{0:T(1024)}) all-reduce(f32[1280]{0:T(1024)S(1)} %copy-done.55, ...), channel_id=1, replica_groups=mesh['shard'=8,'ctx'=2,'tp'=2] {'shard','ctx'}, use_global_device_ids=true, to_apply=%region_31.32 | all-reduce | flops 12160 | bytes 97280 | tf_op jit(solution)/shard_map/psum | solution.py:297
  (707 shorter events, 400.2 us)
Async XLA Ops:
  8.0 50.3 %all-gather.13.cloned.1.call-start = ((), (), s32[]{:S(2)}) async-start(), calls=%async_computation.7 | async-start | bytes 1843200 | tf_op jit(solution)/shard_map/all_gather | solution.py:138
  8.7 152.9 %all-gather.17.cloned.1.call-start = ((), (), s32[]{:S(2)}) async-start(), calls=%async_computation.9 | async-start | bytes 7372800 | tf_op jit(solution)/shard_map/all_gather | solution.py:140
  9.5 234.8 %all-gather.11.cloned.1.call-start = ((), (), s32[]{:S(2)}) async-start(), calls=%async_computation.6 | async-start | bytes 5529600 | tf_op jit(solution)/shard_map/all_gather | solution.py:137
  10.2 336.6 %all-gather.15.cloned.1.call-start = ((), (), s32[]{:S(2)}) async-start(), calls=%async_computation.8 | async-start | bytes 7372800 | tf_op jit(solution)/shard_map/all_gather | solution.py:139
  61.8 285.0 %copy-start = (bf16[2,1,512,1280]{3,2,1,0:T(8,128)(2,1)S(1)}, bf16[2,1,512,1280]{3,2,1,0:T(8,128)(2,1)}, u32[]{:S(2)}) copy-start(bf16[2,1,512,1280]{3,2,1,0:T(8,128)(2,1)} %param.21) | copy-start | bytes 7864324
  61.8 285.0 %copy-start.20 = (f32[1280]{0:T(1024)S(1)}, f32[1280]{0:T(1024)}, u32[]{:S(2)}) copy-start(f32[1280]{0:T(1024)} %param.29) | copy-start | bytes 15364
  61.8 285.0 %copy-start.21 = (f32[1280]{0:T(1024)S(1)}, f32[1280]{0:T(1024)}, u32[]{:S(2)}) copy-start(f32[1280]{0:T(1024)} %param.23) | copy-start | bytes 15364
  61.8 285.0 %copy-start.27 = (f32[1280]{0:T(1024)S(1)}, f32[1280]{0:T(1024)}, u32[]{:S(2)}) copy-start(f32[1280]{0:T(1024)} %param.30) | copy-start | bytes 15364
  61.9 285.0 %copy-start.58 = (f32[1280]{0:T(1024)S(1)}, f32[1280]{0:T(1024)}, u32[]{:S(2)}) copy-start(f32[1280]{0:T(1024)} %param.24) | copy-start | bytes 15364
  61.9 285.0 %copy-start.60 = (f32[1280]{0:T(1024)S(1)}, f32[1280]{0:T(1024)}, u32[]{:S(2)}) copy-start(f32[1280]{0:T(1024)} %param.28) | copy-start | bytes 15364
  61.9 285.0 %copy-start.62 = (f32[2560]{0:T(1024)S(1)}, f32[2560]{0:T(1024)}, u32[]{:S(2)}) copy-start(f32[2560]{0:T(1024)} %param.32) | copy-start | bytes 30724
  347.1 20.5 all-gather.21.cloned.1.call-start
  356.3 19.8 all-gather.19.cloned.1.call-start
  364.5 135.9 %all-reduce.10.cloned.1.call-start = ((), (), s32[]{:S(2)}) async-start(), calls=%async_computation.18 | async-start | bytes 5242880 | tf_op jit(solution)/shard_map/while/body/eval_jaxpr/psum | solution.py:180
  424.7 105.8 %all-gather.25.cloned.1.call-start = ((), (), s32[]{:S(2)}) async-start(), calls=%async_computation.19 | async-start | bytes 7372800 | tf_op jit(solution)/shard_map/while/body/eval_jaxpr/all_gather | solution.py:203
  425.3 207.4 %all-gather.27.cloned.1.call-start = ((), (), s32[]{:S(2)}) async-start(), calls=%async_computation.20 | async-start | bytes 7372800 | tf_op jit(solution)/shard_map/while/body/eval_jaxpr/all_gather | solution.py:202
  425.9 288.3 %all-reduce.12.cloned.1.call-start = ((), (), s32[]{:S(2)}) async-start(), calls=%async_computation.21 | async-start | bytes 5242880 | tf_op jit(solution)/shard_map/while/body/eval_jaxpr/psum | solution.py:217
  641.5 78.4 %all-gather.23.cloned.1.call-start = ((), (), s32[]{:S(2)}) async-start(), calls=%async_computation.17 | async-start | bytes 1843200 | tf_op jit(solution)/shard_map/while/body/eval_jaxpr/all_gather | solution.py:201
  642.1 173.0 %all-reduce.16.cloned.1.call-start = ((), (), s32[]{:S(2)}) async-start(), calls=%async_computation.26 | async-start | bytes 2621440 | tf_op jit(solution)/shard_map/while/body/eval_jaxpr/psum | solution.py:190
  652.8 165.0 %reduce-scatter.15.cloned.1.call-start = ((), (), s32[]{:S(2)}) async-start(), calls=%async_computation.22 | async-start | bytes 3932160 | tf_op jit(solution)/shard_map/while/body/eval_jaxpr/reduce_scatter | solution.py:238
  801.5 24.0 %reduce-scatter.17.cloned.1.call-start = ((), (), s32[]{:S(2)}) async-start(), calls=%async_computation.23 | async-start | bytes 3932160 | tf_op jit(solution)/shard_map/while/body/eval_jaxpr/reduce_scatter | solution.py:237
  802.2 84.8 %all-gather.29.cloned.1.call-start = ((), (), s32[]{:S(2)}) async-start(), calls=%async_computation.24 | async-start | bytes 5529600 | tf_op jit(solution)/shard_map/while/body/eval_jaxpr/all_gather | solution.py:200
  802.9 164.0 %all-reduce.14.cloned.1.call-start = ((), (), s32[]{:S(2)}) async-start(), calls=%async_computation.25 | async-start | bytes 5242880 | tf_op jit(solution)/shard_map/while/body/eval_jaxpr/psum | solution.py:254
  974.7 20.3 all-gather.21.cloned.1.call-start
  983.9 21.7 all-gather.19.cloned.1.call-start
  991.9 137.9 %all-reduce.10.cloned.1.call-start = ((), (), s32[]{:S(2)}) async-start(), calls=%async_computation.18 | async-start | bytes 5242880 | tf_op jit(solution)/shard_map/while/body/eval_jaxpr/psum | solution.py:180
  1054.1 106.1 %all-gather.25.cloned.1.call-start = ((), (), s32[]{:S(2)}) async-start(), calls=%async_computation.19 | async-start | bytes 7372800 | tf_op jit(solution)/shard_map/while/body/eval_jaxpr/all_gather | solution.py:203
  1054.9 207.7 %all-gather.27.cloned.1.call-start = ((), (), s32[]{:S(2)}) async-start(), calls=%async_computation.20 | async-start | bytes 7372800 | tf_op jit(solution)/shard_map/while/body/eval_jaxpr/all_gather | solution.py:202
  1055.6 288.4 %all-reduce.12.cloned.1.call-start = ((), (), s32[]{:S(2)}) async-start(), calls=%async_computation.21 | async-start | bytes 5242880 | tf_op jit(solution)/shard_map/while/body/eval_jaxpr/psum | solution.py:217
  1271.3 78.5 %all-gather.23.cloned.1.call-start = ((), (), s32[]{:S(2)}) async-start(), calls=%async_computation.17 | async-start | bytes 1843200 | tf_op jit(solution)/shard_map/while/body/eval_jaxpr/all_gather | solution.py:201
  1271.9 177.3 %all-reduce.16.cloned.1.call-start = ((), (), s32[]{:S(2)}) async-start(), calls=%async_computation.26 | async-start | bytes 2621440 | tf_op jit(solution)/shard_map/while/body/eval_jaxpr/psum | solution.py:190
  1282.7 169.3 %reduce-scatter.15.cloned.1.call-start = ((), (), s32[]{:S(2)}) async-start(), calls=%async_computation.22 | async-start | bytes 3932160 | tf_op jit(solution)/shard_map/while/body/eval_jaxpr/reduce_scatter | solution.py:238
  1431.5 23.9 %reduce-scatter.17.cloned.1.call-start = ((), (), s32[]{:S(2)}) async-start(), calls=%async_computation.23 | async-start | bytes 3932160 | tf_op jit(solution)/shard_map/while/body/eval_jaxpr/reduce_scatter | solution.py:237
  1432.2 84.4 %all-gather.29.cloned.1.call-start = ((), (), s32[]{:S(2)}) async-start(), calls=%async_computation.24 | async-start | bytes 5529600 | tf_op jit(solution)/shard_map/while/body/eval_jaxpr/all_gather | solution.py:200
  1432.8 163.7 %all-reduce.14.cloned.1.call-start = ((), (), s32[]{:S(2)}) async-start(), calls=%async_computation.25 | async-start | bytes 5242880 | tf_op jit(solution)/shard_map/while/body/eval_jaxpr/psum | solution.py:254
  1606.3 81.0 %reduce-scatter.9.cloned.1.call-start = ((), (), s32[]{:S(2)}) async-start(), calls=%async_computation.11 | async-start | bytes 3686400 | tf_op jit(solution)/shard_map/reduce_scatter | solution.py:304
  1611.0 248.1 %reduce-scatter.7.cloned.1.call-start = ((), (), s32[]{:S(2)}) async-start(), calls=%async_computation.10 | async-start | bytes 11059200 | tf_op jit(solution)/shard_map/reduce_scatter | solution.py:303
  1622.3 454.6 %reduce-scatter.11.cloned.1.call-start = ((), (), s32[]{:S(2)}) async-start(), calls=%async_computation.12 | async-start | bytes 14745600 | tf_op jit(solution)/shard_map/reduce_scatter | solution.py:305
  1623.0 671.5 %reduce-scatter.13.cloned.1.call-start = ((), (), s32[]{:S(2)}) async-start(), calls=%async_computation.13 | async-start | bytes 14745600 | tf_op jit(solution)/shard_map/reduce_scatter | solution.py:306
  1637.1 657.5 %copy-start.32 = (f32[2560]{0:T(1024)S(1)}, f32[2560]{0:T(1024)}, u32[]{:S(2)}) copy-start(f32[2560]{0:T(1024)} %get-tuple-element.1896) | copy-start | bytes 30724
  1637.1 657.5 %copy-start.36 = (f32[3,640]{1,0:T(4,128)S(1)}, f32[3,640]{1,0:T(4,128)}, u32[]{:S(2)}) copy-start(f32[3,640]{1,0:T(4,128)} %get-tuple-element.1892) | copy-start | bytes 23044
  1637.1 657.5 %copy-start.40 = (f32[1280]{0:T(1024)S(1)}, f32[1280]{0:T(1024)}, u32[]{:S(2)}) copy-start(f32[1280]{0:T(1024)} %get-tuple-element.1897) | copy-start | bytes 15364
  1637.1 657.5 %copy-start.43 = (f32[1280]{0:T(1024)S(1)}, f32[1280]{0:T(1024)}, u32[]{:S(2)}) copy-start(f32[1280]{0:T(1024)} %get-tuple-element.1895) | copy-start | bytes 15364
  1637.1 657.5 %copy-start.46 = (f32[1280]{0:T(1024)S(1)}, f32[1280]{0:T(1024)}, u32[]{:S(2)}) copy-start(f32[1280]{0:T(1024)} %get-tuple-element.1894) | copy-start | bytes 15364
  1637.2 657.5 %copy-start.49 = (f32[1280]{0:T(1024)S(1)}, f32[1280]{0:T(1024)}, u32[]{:S(2)}) copy-start(f32[1280]{0:T(1024)} %get-tuple-element.1893) | copy-start | bytes 15364
  1637.2 657.5 %copy-start.52 = (f32[1280]{0:T(1024)S(1)}, f32[1280]{0:T(1024)}, u32[]{:S(2)}) copy-start(f32[1280]{0:T(1024)} %get-tuple-element.1891) | copy-start | bytes 15364
  1637.2 657.5 %copy-start.55 = (f32[1280]{0:T(1024)S(1)}, f32[1280]{0:T(1024)}, u32[]{:S(2)}) copy-start(f32[1280]{0:T(1024)} %get-tuple-element.1890) | copy-start | bytes 15364
  1637.2 718.5 %all-reduce.8.cloned.1.call-start = ((), (), s32[]{:S(2)}) async-start(), calls=%async_computation.14 | async-start | bytes 9830400 | tf_op jit(solution)/shard_map/psum | solution.py:308
  (100 other events, 1115.4 us)
Sparse Core Ops, SparseCore 0:
  11.0 47.2 all-gather.12
  60.5 101.1 all-gather.16
  163.8 80.4 all-gather.10
  246.3 100.4 all-gather.14
  356.4 7.5 all-gather.20
  365.5 10.5 all-gather.18
  424.8 75.5 all-reduce.9
  641.6 72.5 all-reduce.11
  716.6 45.7 all-reduce.15
  801.6 10.0 reduce-scatter.14
  814.0 11.4 reduce-scatter.16
  894.4 72.5 all-reduce.13
  984.0 9.4 all-gather.20
  994.9 10.5 all-gather.18
  1054.2 75.5 all-reduce.9
  1271.5 72.5 all-reduce.11
  1346.3 45.7 all-reduce.15
  1431.6 9.8 reduce-scatter.14
  1443.9 11.4 reduce-scatter.16
  1524.0 72.5 all-reduce.13
  1611.1 76.1 reduce-scatter.8
  1691.3 167.7 reduce-scatter.6
  1863.2 213.6 reduce-scatter.10
  2080.8 213.6 reduce-scatter.12
  2297.6 28.9 all-reduce.7
Sparse Core Ops, SparseCore 1:
  427.4 103.1 all-gather.24
  532.6 100.1 all-gather.26
  644.1 42.9 all-gather.22
  805.2 81.8 all-gather.28
  1057.1 103.1 all-gather.24
  1162.4 100.1 all-gather.26
  1274.0 42.9 all-gather.22
  1434.9 81.6 all-gather.28
where the time goes:
time: 2380 us; the launch traced here: 2370 us
  waiting for transfers between devices  1700 us (71%)
  matrix products  374 us (16%)
  local copies, waits for them, and re-layouts  127 us (5%)
  other arithmetic  73.1 us (3%)
  blocking collectives  61 us (3%)
    reduce_scatter x1, waiting for transfers between devices, per_device(): lax.psum_scatter(weight_grads[2], 'shard', scatter_dimension=0, tiled=True)  218 us
    reduce_scatter x1, waiting for transfers between devices, per_device(): lax.psum_scatter(weight_grads[3], 'shard', scatter_dimension=1, tiled=True)  218 us
    all_gather x2, waiting for transfers between devices, one_micro(): lax.all_gather(fc1_weight, 'shard', axis=0, tiled=True)  181 us
    reduce_scatter x1, waiting for transfers between devices, per_device(): lax.psum_scatter(weight_grads[0], 'shard', scatter_dimension=1, tiled=True)  172 us
    psum x2, waiting for transfers between devices, one_micro(): lax.psum(jnp.dot(mixed, full_proj, preferred_element_type=jnp.float32), '...  148 us
    psum x2, waiting for transfers between devices, one_micro(): lax.psum(jnp.einsum('rf,df->rd', d_pre, back_first, preferred_element_typ...  112 us
    all_gather x2, waiting for transfers between devices, one_micro(): lax.all_gather(qkv_weight, 'shard', axis=1, tiled=True)  111 us
    all_gather x1, waiting for transfers between devices, per_device(): lax.all_gather(fc1_weight, 'shard', axis=0, tiled=True)  103 us
  transfers between devices with their start and end apart: 33, of which 24 were waited for; matrix products, arithmetic and copies ran while one was open for 17% of the time, Pallas kernels for 0%

commit v1 on v0

--- a/solution.py
+++ b/solution.py
@@ -8,6 +8,18 @@
 norm_epsilon = 1e-06
 gelu_factor = 1.702
 rope_base = 10000.0
+
+
+def collect(value, axis, dim):
+    ways, here, step = (lax.axis_size(axis), lax.axis_index(axis), value.shape[dim])
+    line, have = (value, 1)
+    while have < ways:
+        line = jnp.concatenate(
+            [line, lax.ppermute(line, axis, [(d, (d - have) % ways) for d in range(ways)])],
+            axis=dim,
+        )
+        have = 2 * have
+    return jnp.roll(line, here * step, axis=dim)
 
 
 def norm_stats(values):
@@ -134,7 +146,7 @@
     head_count = inner_width // HDIM
     offset = lax.axis_index("ctx") * local_len
     full_qkv, full_proj, full_first, full_second = (
-        lax.all_gather(qkv_weight, "shard", axis=1, tiled=True),
+        collect(qkv_weight, "shard", 1),
         lax.all_gather(proj_weight, "shard", axis=1, tiled=True),
         lax.all_gather(fc1_weight, "shard", axis=0, tiled=True),
         lax.all_gather(fc2_weight, "shard", axis=1, tiled=True),

time: 2380 us -> 2400 us (level)
    ppermute x0 -> x3, waiting for transfers between devices: none -> 240 us  [collect(): lax.ppermute(line, axis, [(d, (d - have) % ways) for d in range(ways)])]
    all_gather x1, waiting for transfers between devices: 99.7 us -> 0.02 us  [per_device(): lax.all_gather(fc2_weight, 'shard', axis=1, tiled=True)]
    all_gather x1 -> x0, waiting for transfers between devices: 73.1 us -> none  [per_device(): lax.all_gather(qkv_weight, 'shard', axis=1, tiled=True)]
    all_gather x1, waiting for transfers between devices: 46.6 us -> 0.01 us  [per_device(): lax.all_gather(proj_weight, 'shard', axis=1, tiled=True)]
    all_gather x1, waiting for transfers between devices: 103 us -> 76.2 us  [per_device(): lax.all_gather(fc1_weight, 'shard', axis=0, tiled=True)]
  transfers between devices with their start and end apart: 33 -> 35, of which waited for: 24 -> 24; matrix products, arithmetic and copies ran while one was open for 17% -> 17% of each run, Pallas kernels for 0% -> 0%
where the time goes in v1:
time: 2400 us; the launch traced here: 2390 us
  waiting for transfers between devices  1700 us (71%)
  matrix products  374 us (16%)
  local copies, waits for them, and re-layouts  145 us (6%)
  other arithmetic  75.8 us (3%)
  blocking collectives  61 us (3%)
    ppermute x3, waiting for transfers between devices, collect(): lax.ppermute(line, axis, [(d, (d - have) % ways) for d in range(ways)])  240 us
    reduce_scatter x1, waiting for transfers between devices, per_device(): lax.psum_scatter(weight_grads[2], 'shard', scatter_dimension=0, tiled=True)  218 us
    reduce_scatter x1, waiting for transfers between devices, per_device(): lax.psum_scatter(weight_grads[3], 'shard', scatter_dimension=1, tiled=True)  218 us
    all_gather x2, waiting for transfers between devices, one_micro(): lax.all_gather(fc1_weight, 'shard', axis=0, tiled=True)  181 us
    reduce_scatter x1, waiting for transfers between devices, per_device(): lax.psum_scatter(weight_grads[0], 'shard', scatter_dimension=1, tiled=True)  172 us
    psum x2, waiting for transfers between devices, one_micro(): lax.psum(jnp.dot(mixed, full_proj, preferred_element_type=jnp.float32), '...  148 us
    psum x2, waiting for transfers between devices, one_micro(): lax.psum(jnp.einsum('rf,df->rd', d_pre, back_first, preferred_element_typ...  122 us
    all_gather x2, waiting for transfers between devices, one_micro(): lax.all_gather(qkv_weight, 'shard', axis=1, tiled=True)  111 us
  transfers between devices with their start and end apart: 35, of which 24 were waited for; matrix products, arithmetic and copies ran while one was open for 17% of the time, Pallas kernels for 0%

profile of v1, /device:TPU:0, one launch (start us, length us, event | category | flops | bytes accessed | tf_op | source)
XLA Modules:
  0.0 2389.1 jit_solution(8228977261901746416)
XLA Ops:
  10.2 6.0 collective-permute-start
  16.3 20.0 collective-permute-done
  37.5 40.4 %collective-permute-done.1 = bf16[3,320,640]{2,1,0:T(8,128)(2,1)S(1)} collective-permute-done((bf16[3,320,640]{2,1,0:T(8,128)(2,1)S(1)}, bf16[3,320,640]{2,1,0:T(8,128)(2,1)S(1)}, u32[]{:S(2)}, u32[]{:S(2)}) %collective-permute-start.1) | collective-permute-done | bytes 1228832 | tf_op jit(solution)/shard_map/ppermute | solution.py:18
  86.2 179.1 %collective-permute-done.2 = bf16[3,640,640]{2,1,0:T(8,128)(2,1)} collective-permute-done((bf16[3,640,640]{2,1,0:T(8,128)(2,1)}, bf16[3,640,640]{2,1,0:T(8,128)(2,1)}, u32[]{:S(2)}, u32[]{:S(2)}) %collective-permute-start.2) | collective-permute-done | bytes 2457632 | tf_op jit(solution)/shard_map/ppermute | solution.py:18
  275.3 5.8 constant_dynamic-slice_fusion.7
  281.1 9.7 copy.94
  290.8 76.2 %all-gather.12.cloned.1.call-done = bf16[1280,2560]{1,0:T(8,128)(2,1)} async-done(((bf16[160,2560]{1,0:T(8,128)(2,1)}), bf16[1280,2560]{1,0:T(8,128)(2,1)}) %all-gather.12.cloned.1.call-update) | async-done | bytes 6553616 | tf_op jit(solution)/shard_map/all_gather | solution.py:151
  367.0 1259.1 %while.96 = (s32[]{:T(128)}, f32[3,1280,640]{1,2,0:T(8,128)}, f32[640,1280]{1,0:T(8,128)}, f32[1280,2560]{1,0:T(8,128)}, f32[2560,1280]{1,0:T(8,128)}, /*index=5...) while((s32[]{:T(128)}, f32[3,1280,640]{1,2,0:T(8,128)}, ...), condition=%wide.region_30.31_spmd.clone, body=%wide.region_0.30_spmd.clone.sunk | while | flops 30925250560 | bytes 610404544 | solution.py:306
  400.4 40.0 %while.97 = (s32[]{:T(128)}, bf16[8,512,80]{1,2,0:T(8,128)(2,1)S(1)}, f32[8,512]{1,0:T(8,128)}, s32[8,512]{1,0:T(8,128)S(1)}, s32[8,1024]{1,0:T(8,128)S(1)}, /*i...) while((s32[]{:T(128)}, ...), condition=%wide.region_6.6_spmd, body=%wide.region_3.5_spmd.sunk | while | flops 172531200 | bytes 7069817 | solution.py:187
  446.6 74.0 %all-reduce.10.cloned.1.call-done = f32[512,1280]{1,0:T(8,128)} async-done(((f32[512,1280]{1,0:T(8,128)}), f32[512,1280]{1,0:T(8,128)}) %all-reduce.10.cloned.1.call-update) | async-done | bytes 2621456 | tf_op jit(solution)/shard_map/while/body/eval_jaxpr/psum | solution.py:192
  523.6 8.4 fusion.165
  531.9 18.7 all-gather.22.cloned.1.call-done
  550.7 11.5 convert_reduce_fusion.10
  562.2 90.6 %all-gather.24.cloned.1.call-done = bf16[1280,2560]{1,0:T(8,128)(2,1)} async-done(((bf16[160,2560]{1,0:T(8,128)(2,1)}), bf16[1280,2560]{1,0:T(8,128)(2,1)}) %all-gather.24.cloned.1.call-update) | async-done | bytes 6553616 | tf_op jit(solution)/shard_map/while/body/eval_jaxpr/all_gather | solution.py:214
  652.8 8.7 fusion.166
  662.3 10.6 convolution_convert_fusion.6
  673.1 61.1 %all-reduce.12.cloned.1.call-done = f32[512,1280]{1,0:T(8,128)} async-done(((f32[512,1280]{1,0:T(8,128)}), f32[512,1280]{1,0:T(8,128)}) %all-reduce.12.cloned.1.call-update) | async-done | bytes 2621456 | tf_op jit(solution)/shard_map/while/body/eval_jaxpr/psum | solution.py:229
  745.8 75.7 %while.98 = (s32[]{:T(128)}, f32[8,512,80]{1,2,0:T(8,128)}, f32[8,1024,80]{1,2,0:T(8,128)}, f32[8,1024,80]{1,2,0:T(8,128)}, s32[8,512]{1,0:T(8,128)S(1)}, /*inde...) while((s32[]{:T(128)}, f32[8,512,80]{1,2,0:T(8,128)}, ...), condition=%wide.region_15.15_spmd, body=%wide.region_13.14_spmd.sunk | while | flops 424795648 | bytes 17794184 | solution.py:242
  823.0 12.0 convolution_add_fusion.8
  851.1 55.9 %all-gather.26.cloned.1.call-done = bf16[3,1280,640]{2,1,0:T(8,128)(2,1)} async-done(((bf16[3,160,640]{2,1,0:T(8,128)(2,1)}), bf16[3,1280,640]{2,1,0:T(8,128)(2,1)}) %all-gather.26.cloned.1.call-update) | async-done | bytes 4915216 | tf_op jit(solution)/shard_map/while/body/eval_jaxpr/all_gather | solution.py:212
  906.9 7.3 convolution_bitcast_fusion.3
  914.3 9.1 convolution_add_fusion.7
  927.4 6.4 bitcast_add_fusion.2
  933.8 53.1 %all-reduce.14.cloned.1.call-done = f32[512,1280]{1,0:T(8,128)} async-done(((f32[512,1280]{1,0:T(8,128)}), f32[512,1280]{1,0:T(8,128)}) %all-reduce.14.cloned.1.call-update) | async-done | bytes 2621456 | tf_op jit(solution)/shard_map/while/body/eval_jaxpr/psum | solution.py:266
  1019.0 6.6 all-gather.16.cloned.1.call-done
  1029.7 40.0 %while.97 = (s32[]{:T(128)}, bf16[8,512,80]{1,2,0:T(8,128)(2,1)S(1)}, f32[8,512]{1,0:T(8,128)}, s32[8,512]{1,0:T(8,128)S(1)}, s32[8,1024]{1,0:T(8,128)S(1)}, /*i...) while((s32[]{:T(128)}, ...), condition=%wide.region_6.6_spmd, body=%wide.region_3.5_spmd.sunk | while | flops 172531200 | bytes 7069817 | solution.py:187
  1075.9 74.0 %all-reduce.10.cloned.1.call-done = f32[512,1280]{1,0:T(8,128)} async-done(((f32[512,1280]{1,0:T(8,128)}), f32[512,1280]{1,0:T(8,128)}) %all-reduce.10.cloned.1.call-update) | async-done | bytes 2621456 | tf_op jit(solution)/shard_map/while/body/eval_jaxpr/psum | solution.py:192
  1152.9 8.4 fusion.165
  1161.2 19.1 all-gather.22.cloned.1.call-done
  1180.3 11.5 convert_reduce_fusion.10
  1191.8 90.8 %all-gather.24.cloned.1.call-done = bf16[1280,2560]{1,0:T(8,128)(2,1)} async-done(((bf16[160,2560]{1,0:T(8,128)(2,1)}), bf16[1280,2560]{1,0:T(8,128)(2,1)}) %all-gather.24.cloned.1.call-update) | async-done | bytes 6553616 | tf_op jit(solution)/shard_map/while/body/eval_jaxpr/all_gather | solution.py:214
  1282.6 8.7 fusion.166
  1292.1 10.6 convolution_convert_fusion.6
  1303.0 61.1 %all-reduce.12.cloned.1.call-done = f32[512,1280]{1,0:T(8,128)} async-done(((f32[512,1280]{1,0:T(8,128)}), f32[512,1280]{1,0:T(8,128)}) %all-reduce.12.cloned.1.call-update) | async-done | bytes 2621456 | tf_op jit(solution)/shard_map/while/body/eval_jaxpr/psum | solution.py:229
  1375.7 75.8 %while.98 = (s32[]{:T(128)}, f32[8,512,80]{1,2,0:T(8,128)}, f32[8,1024,80]{1,2,0:T(8,128)}, f32[8,1024,80]{1,2,0:T(8,128)}, s32[8,512]{1,0:T(8,128)S(1)}, /*inde...) while((s32[]{:T(128)}, f32[8,512,80]{1,2,0:T(8,128)}, ...), condition=%wide.region_15.15_spmd, body=%wide.region_13.14_spmd.sunk | while | flops 424795648 | bytes 17794184 | solution.py:242
  1452.7 16.3 convolution_add_fusion.8
  1480.9 55.6 %all-gather.26.cloned.1.call-done = bf16[3,1280,640]{2,1,0:T(8,128)(2,1)} async-done(((bf16[3,160,640]{2,1,0:T(8,128)(2,1)}), bf16[3,1280,640]{2,1,0:T(8,128)(2,1)}) %all-gather.26.cloned.1.call-update) | async-done | bytes 4915216 | tf_op jit(solution)/shard_map/while/body/eval_jaxpr/all_gather | solution.py:212
  1536.4 7.2 convolution_bitcast_fusion.3
  1543.8 11.9 convolution_add_fusion.7
  1559.7 8.1 bitcast_add_fusion.2
  1567.8 48.6 %all-reduce.14.cloned.1.call-done = f32[512,1280]{1,0:T(8,128)} async-done(((f32[512,1280]{1,0:T(8,128)}), f32[512,1280]{1,0:T(8,128)}) %all-reduce.14.cloned.1.call-update) | async-done | bytes 2621456 | tf_op jit(solution)/shard_map/while/body/eval_jaxpr/psum | solution.py:266
  1630.9 11.3 copy.95
  1643.0 14.0 copy.97
  1657.1 50.0 %reduce-scatter.9.cloned.1.call-done = f32[640,160]{0,1:T(8,128)} async-done(((f32[640,1280]{0,1:T(8,128)}), f32[640,160]{0,1:T(8,128)}) %reduce-scatter.9.cloned.1.call-update) | async-done | bytes 409616 | tf_op jit(solution)/shard_map/reduce_scatter | solution.py:316
  1707.1 172.0 %reduce-scatter.7.cloned.1.call-done = f32[3,160,640]{2,1,0:T(8,128)} async-done(((f32[3,1280,640]{2,1,0:T(8,128)}), f32[3,160,640]{2,1,0:T(8,128)}) %reduce-scatter.7.cloned.1.call-update) | async-done | bytes 1228816 | tf_op jit(solution)/shard_map/reduce_scatter | solution.py:315
  1879.1 217.8 %reduce-scatter.11.cloned.1.call-done = f32[160,2560]{1,0:T(8,128)} async-done(((f32[1280,2560]{1,0:T(8,128)}), f32[160,2560]{1,0:T(8,128)}) %reduce-scatter.11.cloned.1.call-update) | async-done | bytes 1638416 | tf_op jit(solution)/shard_map/reduce_scatter | solution.py:317
  2096.9 217.8 %reduce-scatter.13.cloned.1.call-done = f32[2560,160]{0,1:T(8,128)} async-done(((f32[2560,1280]{0,1:T(8,128)}), f32[2560,160]{0,1:T(8,128)}) %reduce-scatter.13.cloned.1.call-update) | async-done | bytes 1638416 | tf_op jit(solution)/shard_map/reduce_scatter | solution.py:318
  2314.8 61.0 %all-reduce = (f32[1280]{0:T(1024)}, f32[1280]{0:T(1024)}, f32[3,640]{1,0:T(4,128)}, f32[1280]{0:T(1024)}, f32[1280]{0:T(1024)}, /*index=5*/f32[1280]{0:T(1024)}, f32[2560]{0:T(1024)}, f32[1280]{0:T(1024)}) all-reduce(f32[1280]{0:T(1024)S(1)} %copy-done.56, ...), channel_id=1, replica_groups=mesh['shard'=8,'ctx'=2,'tp'=2] {'shard','ctx'}, use_global_device_ids=true, to_apply=%region_31.32 | all-reduce | flops 12160 | bytes 97280 | tf_op jit(solution)/shard_map/psum | solution.py:309
  (725 shorter events, 420.1 us)
Async XLA Ops:
  8.0 74.7 %all-gather.10.cloned.1.call-start = ((), (), s32[]{:S(2)}) async-start(), calls=%async_computation.6 | async-start | bytes 1843200 | tf_op jit(solution)/shard_map/all_gather | solution.py:150
  8.8 272.4 %all-gather.14.cloned.1.call-start = ((), (), s32[]{:S(2)}) async-start(), calls=%async_computation.8 | async-start | bytes 7372800 | tf_op jit(solution)/shard_map/all_gather | solution.py:152
  9.5 357.5 %all-gather.12.cloned.1.call-start = ((), (), s32[]{:S(2)}) async-start(), calls=%async_computation.7 | async-start | bytes 7372800 | tf_op jit(solution)/shard_map/all_gather | solution.py:151
  10.2 26.0 %collective-permute-start = (bf16[3,160,640]{2,1,0:T(8,128)(2,1)}, bf16[3,160,640]{2,1,0:T(8,128)(2,1)S(1)}, u32[]{:S(2)}, u32[]{:S(2)}) collective-permute-start(bf16[3,160,640]{2,1,0:T(8,128)(2,1)} %param.25), channel_id=1, source_target_pairs={{0,28},{4,0},{8,4},{12,8},{16,12},{20,16},{24,20},{28,24},{1,29},{... | collective-permute-start | bytes 1843208 | tf_op jit(solution)/shard_map/ppermute | solution.py:18
  37.5 40.5 %collective-permute-start.1 = (bf16[3,320,640]{2,1,0:T(8,128)(2,1)S(1)}, bf16[3,320,640]{2,1,0:T(8,128)(2,1)S(1)}, u32[]{:S(2)}, u32[]{:S(2)}) collective-permute-start(bf16[3,320,640]{2,1,0:T(8,128)(2,1)S(1)} %pad_maximum_fusion.7), channel_id=1, source_target_pairs={{0,24},{4,28},{8,0},{12,4},{16,8},{20,12},{24,16},{28,20},{1,25},{... | collective-permute-start | bytes 3686408 | tf_op jit(solution)/shard_map/ppermute | solution.py:18
  79.6 185.8 %collective-permute-start.2 = (bf16[3,640,640]{2,1,0:T(8,128)(2,1)}, bf16[3,640,640]{2,1,0:T(8,128)(2,1)}, u32[]{:S(2)}, u32[]{:S(2)}) collective-permute-start(bf16[3,640,640]{2,1,0:T(8,128)(2,1)} %pad_maximum_fusion.6), channel_id=1, source_target_pairs={{0,16},{4,20},{8,24},{12,28},{16,0},{20,4},{24,8},{28,12},{1,17},{... | collective-permute-start | bytes 7372808 | tf_op jit(solution)/shard_map/ppermute | solution.py:18
  281.0 85.9 %copy-start = (bf16[2,1,512,1280]{3,2,1,0:T(8,128)(2,1)S(1)}, bf16[2,1,512,1280]{3,2,1,0:T(8,128)(2,1)}, u32[]{:S(2)}) copy-start(bf16[2,1,512,1280]{3,2,1,0:T(8,128)(2,1)} %param.21) | copy-start | bytes 7864324
  281.1 85.9 %copy-start.21 = (f32[1280]{0:T(1024)S(1)}, f32[1280]{0:T(1024)}, u32[]{:S(2)}) copy-start(f32[1280]{0:T(1024)} %param.29) | copy-start | bytes 15364
  281.1 85.9 %copy-start.22 = (f32[1280]{0:T(1024)S(1)}, f32[1280]{0:T(1024)}, u32[]{:S(2)}) copy-start(f32[1280]{0:T(1024)} %param.23) | copy-start | bytes 15364
  281.1 85.9 %copy-start.28 = (f32[1280]{0:T(1024)S(1)}, f32[1280]{0:T(1024)}, u32[]{:S(2)}) copy-start(f32[1280]{0:T(1024)} %param.30) | copy-start | bytes 15364
  281.1 85.9 %copy-start.59 = (f32[1280]{0:T(1024)S(1)}, f32[1280]{0:T(1024)}, u32[]{:S(2)}) copy-start(f32[1280]{0:T(1024)} %param.24) | copy-start | bytes 15364
  367.3 20.5 all-gather.18.cloned.1.call-start
  376.5 19.8 all-gather.16.cloned.1.call-start
  384.7 135.9 %all-reduce.10.cloned.1.call-start = ((), (), s32[]{:S(2)}) async-start(), calls=%async_computation.17 | async-start | bytes 5242880 | tf_op jit(solution)/shard_map/while/body/eval_jaxpr/psum | solution.py:192
  444.9 105.8 %all-gather.22.cloned.1.call-start = ((), (), s32[]{:S(2)}) async-start(), calls=%async_computation.18 | async-start | bytes 7372800 | tf_op jit(solution)/shard_map/while/body/eval_jaxpr/all_gather | solution.py:215
  445.5 207.4 %all-gather.24.cloned.1.call-start = ((), (), s32[]{:S(2)}) async-start(), calls=%async_computation.19 | async-start | bytes 7372800 | tf_op jit(solution)/shard_map/while/body/eval_jaxpr/all_gather | solution.py:214
  446.0 288.2 %all-reduce.12.cloned.1.call-start = ((), (), s32[]{:S(2)}) async-start(), calls=%async_computation.20 | async-start | bytes 5242880 | tf_op jit(solution)/shard_map/while/body/eval_jaxpr/psum | solution.py:229
  661.6 78.4 %all-gather.20.cloned.1.call-start = ((), (), s32[]{:S(2)}) async-start(), calls=%async_computation.16 | async-start | bytes 1843200 | tf_op jit(solution)/shard_map/while/body/eval_jaxpr/all_gather | solution.py:213
  662.2 172.8 %all-reduce.16.cloned.1.call-start = ((), (), s32[]{:S(2)}) async-start(), calls=%async_computation.25 | async-start | bytes 2621440 | tf_op jit(solution)/shard_map/while/body/eval_jaxpr/psum | solution.py:202
  672.9 164.8 %reduce-scatter.15.cloned.1.call-start = ((), (), s32[]{:S(2)}) async-start(), calls=%async_computation.21 | async-start | bytes 3932160 | tf_op jit(solution)/shard_map/while/body/eval_jaxpr/reduce_scatter | solution.py:250
  821.6 23.9 reduce-scatter.17.cloned.1.call-start
  822.1 84.8 %all-gather.26.cloned.1.call-start = ((), (), s32[]{:S(2)}) async-start(), calls=%async_computation.23 | async-start | bytes 5529600 | tf_op jit(solution)/shard_map/while/body/eval_jaxpr/all_gather | solution.py:212
  822.9 164.0 %all-reduce.14.cloned.1.call-start = ((), (), s32[]{:S(2)}) async-start(), calls=%async_computation.24 | async-start | bytes 5242880 | tf_op jit(solution)/shard_map/while/body/eval_jaxpr/psum | solution.py:266
  994.6 20.3 all-gather.18.cloned.1.call-start
  1003.8 21.8 all-gather.16.cloned.1.call-start
  1011.8 138.1 %all-reduce.10.cloned.1.call-start = ((), (), s32[]{:S(2)}) async-start(), calls=%async_computation.17 | async-start | bytes 5242880 | tf_op jit(solution)/shard_map/while/body/eval_jaxpr/psum | solution.py:192
  1074.2 106.1 %all-gather.22.cloned.1.call-start = ((), (), s32[]{:S(2)}) async-start(), calls=%async_computation.18 | async-start | bytes 7372800 | tf_op jit(solution)/shard_map/while/body/eval_jaxpr/all_gather | solution.py:215
  1074.9 207.7 %all-gather.24.cloned.1.call-start = ((), (), s32[]{:S(2)}) async-start(), calls=%async_computation.19 | async-start | bytes 7372800 | tf_op jit(solution)/shard_map/while/body/eval_jaxpr/all_gather | solution.py:214
  1075.7 288.4 %all-reduce.12.cloned.1.call-start = ((), (), s32[]{:S(2)}) async-start(), calls=%async_computation.20 | async-start | bytes 5242880 | tf_op jit(solution)/shard_map/while/body/eval_jaxpr/psum | solution.py:229
  1291.4 78.4 %all-gather.20.cloned.1.call-start = ((), (), s32[]{:S(2)}) async-start(), calls=%async_computation.16 | async-start | bytes 1843200 | tf_op jit(solution)/shard_map/while/body/eval_jaxpr/all_gather | solution.py:213
  1292.0 177.0 %all-reduce.16.cloned.1.call-start = ((), (), s32[]{:S(2)}) async-start(), calls=%async_computation.25 | async-start | bytes 2621440 | tf_op jit(solution)/shard_map/while/body/eval_jaxpr/psum | solution.py:202
  1302.7 169.0 %reduce-scatter.15.cloned.1.call-start = ((), (), s32[]{:S(2)}) async-start(), calls=%async_computation.21 | async-start | bytes 3932160 | tf_op jit(solution)/shard_map/while/body/eval_jaxpr/reduce_scatter | solution.py:250
  1451.5 23.7 reduce-scatter.17.cloned.1.call-start
  1452.1 84.4 %all-gather.26.cloned.1.call-start = ((), (), s32[]{:S(2)}) async-start(), calls=%async_computation.23 | async-start | bytes 5529600 | tf_op jit(solution)/shard_map/while/body/eval_jaxpr/all_gather | solution.py:212
  1452.7 163.7 %all-reduce.14.cloned.1.call-start = ((), (), s32[]{:S(2)}) async-start(), calls=%async_computation.24 | async-start | bytes 5242880 | tf_op jit(solution)/shard_map/while/body/eval_jaxpr/psum | solution.py:266
  1626.1 81.0 %reduce-scatter.9.cloned.1.call-start = ((), (), s32[]{:S(2)}) async-start(), calls=%async_computation.10 | async-start | bytes 3686400 | tf_op jit(solution)/shard_map/reduce_scatter | solution.py:316
  1630.8 248.3 %reduce-scatter.7.cloned.1.call-start = ((), (), s32[]{:S(2)}) async-start(), calls=%async_computation.9 | async-start | bytes 11059200 | tf_op jit(solution)/shard_map/reduce_scatter | solution.py:315
  1642.2 454.8 %reduce-scatter.11.cloned.1.call-start = ((), (), s32[]{:S(2)}) async-start(), calls=%async_computation.11 | async-start | bytes 14745600 | tf_op jit(solution)/shard_map/reduce_scatter | solution.py:317
  1642.9 671.8 %reduce-scatter.13.cloned.1.call-start = ((), (), s32[]{:S(2)}) async-start(), calls=%async_computation.12 | async-start | bytes 14745600 | tf_op jit(solution)/shard_map/reduce_scatter | solution.py:318
  1657.0 657.7 %copy-start.33 = (f32[2560]{0:T(1024)S(1)}, f32[2560]{0:T(1024)}, u32[]{:S(2)}) copy-start(f32[2560]{0:T(1024)} %get-tuple-element.1896) | copy-start | bytes 30724
  1657.0 657.7 %copy-start.37 = (f32[3,640]{1,0:T(4,128)S(1)}, f32[3,640]{1,0:T(4,128)}, u32[]{:S(2)}) copy-start(f32[3,640]{1,0:T(4,128)} %get-tuple-element.1892) | copy-start | bytes 23044
  1657.0 657.7 %copy-start.41 = (f32[1280]{0:T(1024)S(1)}, f32[1280]{0:T(1024)}, u32[]{:S(2)}) copy-start(f32[1280]{0:T(1024)} %get-tuple-element.1897) | copy-start | bytes 15364
  1657.0 657.7 %copy-start.44 = (f32[1280]{0:T(1024)S(1)}, f32[1280]{0:T(1024)}, u32[]{:S(2)}) copy-start(f32[1280]{0:T(1024)} %get-tuple-element.1895) | copy-start | bytes 15364
  1657.0 657.7 %copy-start.47 = (f32[1280]{0:T(1024)S(1)}, f32[1280]{0:T(1024)}, u32[]{:S(2)}) copy-start(f32[1280]{0:T(1024)} %get-tuple-element.1894) | copy-start | bytes 15364
  1657.0 657.7 %copy-start.50 = (f32[1280]{0:T(1024)S(1)}, f32[1280]{0:T(1024)}, u32[]{:S(2)}) copy-start(f32[1280]{0:T(1024)} %get-tuple-element.1893) | copy-start | bytes 15364
  1657.0 657.7 %copy-start.53 = (f32[1280]{0:T(1024)S(1)}, f32[1280]{0:T(1024)}, u32[]{:S(2)}) copy-start(f32[1280]{0:T(1024)} %get-tuple-element.1891) | copy-start | bytes 15364
  1657.1 657.7 %copy-start.56 = (f32[1280]{0:T(1024)S(1)}, f32[1280]{0:T(1024)}, u32[]{:S(2)}) copy-start(f32[1280]{0:T(1024)} %get-tuple-element.1890) | copy-start | bytes 15364
  1657.1 718.7 %all-reduce.8.cloned.1.call-start = ((), (), s32[]{:S(2)}) async-start(), calls=%async_computation.13 | async-start | bytes 9830400 | tf_op jit(solution)/shard_map/psum | solution.py:320
  (104 other events, 1200.9 us)
Sparse Core Ops, SparseCore 0:
  11.0 57.5 all-gather.9
  70.9 192.6 all-gather.13
  265.7 101.2 all-gather.11
  376.6 7.5 all-gather.17
  385.7 10.5 all-gather.15
  445.0 75.5 all-reduce.9
  661.7 72.5 all-reduce.11
  736.7 45.7 all-reduce.15
  821.7 10.0 reduce-scatter.14
  833.9 11.4 reduce-scatter.16
  914.3 72.5 all-reduce.13
  1004.0 9.3 all-gather.17
  1015.0 10.5 all-gather.15
  1074.3 75.5 all-reduce.9
  1291.5 72.5 all-reduce.11
  1366.3 45.7 all-reduce.15
  1451.6 9.9 reduce-scatter.14
  1463.8 11.3 reduce-scatter.16
  1543.8 72.5 all-reduce.13
  1630.9 76.1 reduce-scatter.8
  1711.2 167.9 reduce-scatter.6
  1883.2 213.6 reduce-scatter.10
  2101.0 213.6 reduce-scatter.12
  2317.6 28.9 all-reduce.7
Sparse Core Ops, SparseCore 1:
  447.5 103.1 all-gather.21
  552.7 100.1 all-gather.23
  664.3 42.9 all-gather.19
  825.1 81.8 all-gather.25
  1077.2 103.1 all-gather.21
  1182.5 100.1 all-gather.23
  1294.1 42.9 all-gather.19
  1454.7 81.6 all-gather.25
